TPU v7x, 32 devices: a whole 2x2x4 slice. The times are simulated.
32 devices in a mesh: stn: 2 (over x), vox: 16 (over z, y, core).
Axes of the slice: x: 2, y: 2, z: 4, core: 2. Of those that a mesh axis runs over, the one named last changes fastest.
Arguments:
- voltages: bfloat16 [56, 2, 65536], P('stn', None, 'vox'), may hold values from -6 to 6
- sample_delays: int32 [56, 65536], P(None, 'vox'), may hold values from 0 to 239
- timing_offsets: int32 [56], replicated, may hold values from 0 to 15
- reference_station: int32 [1], replicated, may hold values from 0 to 55
Outputs:
- image_out: float32 [64, 65536], P('stn', 'vox')
All inputs are finite; a program needn't handle non-finite values.
Results may differ from a plain program's by a relative error of at most 0.004.
Values may be sent and summed in bfloat16 or wider, within the bound.
No kernel may reach another device: no remote copies, remote signals or barrier semaphores. Data moves between devices by JAX's collectives and lax.ppermute only.
A program may use at most 64 MiB of HBM per device.

v0:
```python
import math
import jax
import jax.numpy as jnp
from jax import lax
from jax.sharding import PartitionSpec as P

STATIONS = 56
WIN = 1024
LAGS = 256


def spread(value, axis, source):
    kept = jnp.where(lax.axis_index(axis) == source, value, 0).astype(value.dtype)
    return lax.psum(kept, axis)


def padded(block, sides, width):
    for axis, dim in sides:
        count = lax.axis_size(axis)
        forward = [(i, i + 1) for i in range(count - 1)]
        backward = [(target, source) for source, target in forward]
        low = lax.ppermute(
            lax.slice_in_dim(block, block.shape[dim] - width, None, axis=dim), axis, forward
        )
        high = lax.ppermute(lax.slice_in_dim(block, 0, width, axis=dim), axis, backward)
        block = jnp.concatenate([low, block, high], axis=dim)
    return block


def taper_weights(length):
    position = (jnp.arange(length, dtype=jnp.float32) + 0.5) / length
    return 0.5 - 0.5 * jnp.cos(2.0 * math.pi * position)


def shards(voltages, sample_delays, timing_offsets, reference_station):
    stations_here, polarizations, samples_here = voltages.shape
    slices_here = samples_here // WIN
    voxels_here = sample_delays.shape[1]
    station_ref = reference_station[0]
    stn_index = lax.axis_index("stn")
    taper_curve = taper_weights(WIN)
    norm_inv = 1.0 / jnp.sqrt(jnp.sum(taper_curve * taper_curve))
    owner_index = station_ref // stations_here
    ref_local = lax.dynamic_index_in_dim(voltages, station_ref % stations_here, 0, keepdims=False)
    ref_signal = spread(ref_local, "stn", owner_index)
    extended = padded(ref_signal, (("vox", 1),), LAGS // 2)
    extended = jnp.pad(extended, ((0, 0), (0, WIN)))
    leading = extended[:, :samples_here].reshape(polarizations, slices_here, WIN)
    trailing = extended[:, WIN : samples_here + WIN].reshape(polarizations, slices_here, WIN)[
        :, :, : LAGS - 1
    ]
    segments = jnp.concatenate([leading, trailing], axis=2).reshape(
        1, polarizations * slices_here, WIN + LAGS - 1
    )
    windowed = (
        voltages.reshape(stations_here, polarizations, slices_here, WIN) * taper_curve
    ).astype(jnp.bfloat16)
    kernels = jnp.transpose(windowed, (1, 2, 0, 3)).reshape(
        polarizations * slices_here * stations_here, 1, WIN
    )
    lagged_sums = lax.conv_general_dilated(
        segments,
        kernels,
        (1,),
        "VALID",
        feature_group_count=polarizations * slices_here,
        preferred_element_type=jnp.float32,
    )
    lagged_sums = jnp.sum(
        lagged_sums.reshape(polarizations, slices_here, stations_here, LAGS), axis=0
    )
    station_ids = stn_index * stations_here + jnp.arange(stations_here, dtype=jnp.int32)
    keep_mask = (station_ids != station_ref).astype(jnp.float32)
    local_corr = (
        jnp.transpose(lagged_sums, (1, 0, 2)) * keep_mask[:, None, None] * norm_inv
    ).astype(jnp.bfloat16)
    corr_all = lax.all_gather(local_corr, "vox", axis=1, tiled=True)
    lag_index = sample_delays + timing_offsets[:, None]
    total_slices = corr_all.shape[1]
    out_scale = 1.0 / math.sqrt(2.0 * STATIONS)
    my_lags = lax.dynamic_slice_in_dim(lag_index, stn_index * stations_here, stations_here, 0)
    corr_block = lax.slice_in_dim(
        corr_all, 0, lax.axis_size("stn") * (total_slices // lax.axis_size("stn")), axis=1
    )
    lag_grid = lax.broadcasted_iota(jnp.int32, (LAGS, voxels_here), 0)

    def add_station(running, inputs_pair):
        corr_rows, lags_one = inputs_pair
        selector = (lag_grid == lags_one[None, :]).astype(jnp.bfloat16)
        return (running + jnp.dot(corr_rows, selector, preferred_element_type=jnp.float32), None)

    running, unused = lax.scan(
        add_station,
        jnp.zeros(
            (lax.axis_size("stn") * (total_slices // lax.axis_size("stn")), voxels_here),
            jnp.float32,
        ),
        (corr_block, my_lags),
    )
    image_out = lax.psum_scatter(running, "stn", scatter_dimension=0, tiled=True)
    return image_out * out_scale


def solution(mesh):
    return jax.shard_map(
        shards,
        mesh=mesh,
        in_specs=(P("stn", None, "vox"), P(None, "vox"), P(), P()),
        out_specs=P("stn", "vox"),
        check_vma=False,
    )
```

profile of v0, /device:TPU:0, one launch (start us, length us, event | category | flops | bytes accessed | tf_op | source)
XLA Modules:
  0.0 126.3 jit_solution(5938789996437528588)
XLA Ops:
  8.0 9.7 %psum.7 = bf16[2,4096]{1,0:T(2,128)(2,1)S(1)} all-reduce(bf16[2,4096]{1,0:T(2,128)(2,1)S(1)} %fusion.14), channel_id=1, replica_groups=mesh['stn'=2,'vox'=16] {'stn'}, use_global_device_ids=true, to_apply=%region_0.0 | all-reduce | flops 8192 | bytes 32768 | tf_op jit(solution)/shard_map/psum | solution.py:14
  17.6 1.3 %collective-permute-start = (bf16[2,128]{1,0:T(2,128)(2,1)S(1)}, bf16[2,128]{1,0:T(2,128)(2,1)S(1)}, u32[]{:S(2)}, u32[]{:S(2)}) collective-permute-start(bf16[2,128]{1,0:T(2,128)(2,1)S(1)} %get-tuple-element.64), channel_id=1, source_target_pairs={{0,1},{1,2},{2,3},{3,4},{4,5},{5,6},{6,7},{7,8},{8,9},{9,10},{10,1... | collective-permute-start | bytes 1544 | tf_op jit(solution)/shard_map/ppermute | solution.py:22
  18.9 1.3 %collective-permute-start.1 = (bf16[2,128]{1,0:T(2,128)(2,1)S(1)}, bf16[2,128]{1,0:T(2,128)(2,1)S(1)}, u32[]{:S(2)}, u32[]{:S(2)}) collective-permute-start(bf16[2,128]{1,0:T(2,128)(2,1)S(1)} %get-tuple-element.65), channel_id=1, source_target_pairs={{1,0},{2,1},{3,2},{4,3},{5,4},{6,5},{7,6},{8,7},{9,8},{10,9},{11,1... | collective-permute-start | bytes 1544 | tf_op jit(solution)/shard_map/ppermute | solution.py:25
  20.2 1.4 %reshape.40 = f32[28,2,4,1024]{3,2,1,0:T(4,128)S(1)} reshape(bf16[28,2,4096]{2,1,0:T(2,128)(2,1)} %param.6) | data formatting | bytes 1376256 | tf_op jit(solution)/shard_map/convert_element_type | solution.py:56
  25.6 16.9 %fusion.7 = f32[1,224,256]{1,0,2:T(1,128)S(1)} fusion(bf16[1,8,1279]{1,0,2:T(2,128)(2,1)S(1)} %copy.13, s32[224]{0:T(256)S(1)} %copy-done.3, bf16[224,1024]{0,1:T(8,128)(2,1)S(1)} %copy.12), kind=kOutput, calls=%fused_computation.10 | convolution fusion | flops 943194112 | bytes 709488 | tf_op jit(solution)/shard_map/conv_general_dilated | solution.py:61
  42.8 27.5 %all_gather.3 = bf16[28,64,256]{2,0,1:T(8,128)(2,1)S(1)} all-gather(bf16[28,4,256]{2,0,1:T(8,128)(2,1)S(1)} %fusion.13), channel_id=1, replica_groups=mesh['stn'=2,'vox'=16] {'vox'}, dimensions={1}, use_global_device_ids=true | all-gather | bytes 974848 | tf_op jit(solution)/shard_map/all_gather | solution.py:77
  70.9 28.9 %while.11 = (s32[]{:T(128)}, f32[64,4096]{1,0:T(8,128)S(1)}, bf16[28,64,256]{2,1,0:T(8,128)(2,1)S(1)}, s32[28,4096]{1,0:T(8,128)S(1)}, s32[]{:T(128)}, /*index=5*/s32[]{:T(128)}) while((s32[]{:T(128)}, f32[64,4096]{1,0:T(8,128)S(1)}, bf16[28,64,256]{2,1,0:T(8,128)(2,1)S(1)}, s32[28,4096]{1,0:T(8,128)S(1)}, s32[]{:T(128)}, ...), condition=%wide.region_4.5_spmd.clone, body=%wide.region_3.4_spmd.clone.sunk | while | flops 135790592 | bytes 2179159 | solution.py:92
  70.9 1.0 convolution_add_fusion.2
  73.0 1.0 convolution_add_fusion.2
  75.1 1.0 convolution_add_fusion.2
  77.1 1.0 convolution_add_fusion.2
  79.2 1.0 convolution_add_fusion.2
  81.2 1.0 convolution_add_fusion.2
  83.3 1.0 convolution_add_fusion.2
  85.4 1.0 convolution_add_fusion.2
  87.4 1.0 convolution_add_fusion.2
  89.5 1.0 convolution_add_fusion.2
  91.6 1.0 convolution_add_fusion.2
  93.6 1.0 convolution_add_fusion.2
  95.7 1.0 convolution_add_fusion.2
  97.7 1.0 convolution_add_fusion.2
  99.8 1.0 copy-done
  100.8 16.8 %reduce-scatter.2.cloned.1.call-done = f32[32,4096]{1,0:T(8,128)} async-done(((f32[64,4096]{1,0:T(8,128)}), f32[32,4096]{1,0:T(8,128)}) %reduce-scatter.2.cloned.1.call-update) | async-done | bytes 524304 | tf_op jit(solution)/shard_map/reduce_scatter | solution.py:100
  117.6 1.9 %broadcast_multiply_fusion = f32[32,4096]{1,0:T(8,128)} fusion(f32[32,4096]{1,0:T(8,128)} %reduce-scatter.2.cloned.1.call-done), kind=kLoop, calls=%fused_computation.17 | loop fusion | flops 131072 | bytes 1048576 | tf_op jit(solution)/shard_map/mul | solution.py:101
  (76 shorter events, 19.0 us)
Async XLA Ops:
  6.5 111.1 %reduce-scatter.2.cloned.1.call-start = ((), (), s32[]{:S(2)}) async-start(), calls=%async_computation.1 | async-start | bytes 1572864 | tf_op jit(solution)/shard_map/reduce_scatter | solution.py:100
  17.6 6.9 %collective-permute-start = (bf16[2,128]{1,0:T(2,128)(2,1)S(1)}, bf16[2,128]{1,0:T(2,128)(2,1)S(1)}, u32[]{:S(2)}, u32[]{:S(2)}) collective-permute-start(bf16[2,128]{1,0:T(2,128)(2,1)S(1)} %get-tuple-element.64), channel_id=1, source_target_pairs={{0,1},{1,2},{2,3},{3,4},{4,5},{5,6},{6,7},{7,8},{8,9},{9,10},{10,1... | collective-permute-start | bytes 1544 | tf_op jit(solution)/shard_map/ppermute | solution.py:22
  18.9 5.6 %collective-permute-start.1 = (bf16[2,128]{1,0:T(2,128)(2,1)S(1)}, bf16[2,128]{1,0:T(2,128)(2,1)S(1)}, u32[]{:S(2)}, u32[]{:S(2)}) collective-permute-start(bf16[2,128]{1,0:T(2,128)(2,1)S(1)} %get-tuple-element.65), channel_id=1, source_target_pairs={{1,0},{2,1},{3,2},{4,3},{5,4},{6,5},{7,6},{8,7},{9,8},{10,9},{11,1... | collective-permute-start | bytes 1544 | tf_op jit(solution)/shard_map/ppermute | solution.py:25
  21.7 0.7 copy-start.2
  21.7 1.2 copy-start.1
  23.1 2.5 %copy-start.3 = (s32[224]{0:T(256)S(1)}, s32[224]{0:T(256)}, u32[]{:S(2)}) copy-start(s32[224]{0:T(256)} %constant.54.clone.1) | copy-start | bytes 2692
  99.8 1.0 copy-start
Sparse Core Ops, SparseCore 0:
  100.9 16.6 reduce-scatter.1
where the time goes:
time: 127 us; the launch traced here: 126 us
  matrix products  44.3 us (35%)
  blocking collectives  37.2 us (29%)
  waiting for transfers between devices  16.8 us (13%)
  between operations  14.9 us (12%)
  local copies, waits for them, and re-layouts  5.49 us (4%)
  other arithmetic  4.06 us (3%)
  starting transfers between devices  2.58 us (2%)
    all_gather x1, blocking collectives, shards(): corr_all = lax.all_gather(local_corr, 'vox', axis=1, tiled=True)  27.5 us
    dot_general x28, matrix products, add_station(): jnp.dot(corr_rows, selector, preferred_element_type=jnp.float32)  27.4 us
    conv_general_dilated x1, matrix products, shards(): lax.conv_general_dilated(segments, kernels, (1,), 'VALID', feature_group_...  16.9 us
    reduce_scatter x1, waiting for transfers between devices, shards(): lax.psum_scatter(running, 'stn', scatter_dimension=0, tiled=True)  16.8 us
    psum x1, blocking collectives, spread(): return lax.psum(kept, axis)  9.65 us
  transfers between devices with their start and end apart: 3, of which 1 were waited for; matrix products, arithmetic and copies ran while one was open for 2% of the time, Pallas kernels for 0%

commit v1 on v0

--- a/solution.py
+++ b/solution.py
@@ -7,6 +7,19 @@
 STATIONS = 56
 WIN = 1024
 LAGS = 256
+
+
+def gather_around(x, axis, dim):
+    ways = lax.axis_size(axis)
+    up = [(d, (d + 1) % ways) for d in range(ways)]
+    down = [(d, (d - 1) % ways) for d in range(ways)]
+    earlier, later = ([x], [x])
+    for _ in range(ways // 2):
+        earlier.append(lax.ppermute(earlier[-1], axis, up))
+    for _ in range((ways - 1) // 2):
+        later.append(lax.ppermute(later[-1], axis, down))
+    line = jnp.concatenate([*earlier[::-1], *later[1:]], axis=dim)
+    return jnp.roll(line, (lax.axis_index(axis) - ways // 2) * x.shape[dim], axis=dim)
 
 
 def spread(value, axis, source):
@@ -74,7 +87,7 @@
     local_corr = (
         jnp.transpose(lagged_sums, (1, 0, 2)) * keep_mask[:, None, None] * norm_inv
     ).astype(jnp.bfloat16)
-    corr_all = lax.all_gather(local_corr, "vox", axis=1, tiled=True)
+    corr_all = gather_around(local_corr, "vox", 1)
     lag_index = sample_delays + timing_offsets[:, None]
     total_slices = corr_all.shape[1]
     out_scale = 1.0 / math.sqrt(2.0 * STATIONS)

time: 127 us -> 155 us (1.22)
  starting transfers between devices: 2.58 us -> 36.8 us
  blocking collectives: 37.2 us -> 9.65 us
  waiting for transfers between devices: 16.8 us -> 38.7 us
    ppermute x0 -> x15, starting transfers between devices: none -> 34.2 us  [the longest x7 31.3 us: gather_around(): later.append(lax.ppermute(later[-1], axis, down))]
    all_gather x1 -> x0, blocking collectives: 27.5 us -> none  [shards(): corr_all = lax.all_gather(local_corr, 'vox', axis=1, tiled=True)]
    ppermute x0 -> x15, waiting for transfers between devices: none -> 18.1 us  [the longest x8 18 us: gather_around(): earlier.append(lax.ppermute(earlier[-1], axis, up))]
    reduce_scatter x1, waiting for transfers between devices: 16.8 us -> 20.6 us  [shards(): lax.psum_scatter(running, 'stn', scatter_dimension=0, tiled=True)]
  transfers between devices with their start and end apart: 3 -> 18, of which waited for: 1 -> 9; matrix products, arithmetic and copies ran while one was open for 2% -> 2% of each run, Pallas kernels for 0% -> 0%
where the time goes in v1:
time: 155 us
  matrix products  44.2 us (29%)
  waiting for transfers between devices  38.7 us (25%)
  starting transfers between devices  36.8 us (24%)
  between operations  15.3 us (10%)
  blocking collectives  9.65 us (6%)
  local copies, waits for them, and re-layouts  5.05 us (3%)
  other arithmetic  4.23 us (3%)
    ppermute x7, starting transfers between devices, gather_around(): later.append(lax.ppermute(later[-1], axis, down))  31.3 us
    dot_general x28, matrix products, add_station(): jnp.dot(corr_rows, selector, preferred_element_type=jnp.float32)  27.4 us
    reduce_scatter x1, waiting for transfers between devices, shards(): lax.psum_scatter(running, 'stn', scatter_dimension=0, tiled=True)  20.6 us
    ppermute x8, waiting for transfers between devices, gather_around(): earlier.append(lax.ppermute(earlier[-1], axis, up))  18 us
    conv_general_dilated x1, matrix products, shards(): lax.conv_general_dilated(segments, kernels, (1,), 'VALID', feature_group_...  16.9 us
    psum x1, blocking collectives, spread(): return lax.psum(kept, axis)  9.65 us
  transfers between devices with their start and end apart: 18, of which 9 were waited for; matrix products, arithmetic and copies ran while one was open for 2% of the time, Pallas kernels for 0%

profile of v1, /device:TPU:0, one launch (start us, length us, event | category | flops | bytes accessed | tf_op | source)
XLA Modules:
  0.0 155.0 jit_solution(6300618414055516323)
XLA Ops:
  8.0 9.7 %psum.7 = bf16[2,4096]{1,0:T(2,128)(2,1)S(1)} all-reduce(bf16[2,4096]{1,0:T(2,128)(2,1)S(1)} %fusion.14), channel_id=1, replica_groups=mesh['stn'=2,'vox'=16] {'stn'}, use_global_device_ids=true, to_apply=%region_0.0 | all-reduce | flops 8192 | bytes 32768 | tf_op jit(solution)/shard_map/psum | solution.py:27
  17.6 1.3 collective-permute-start
  18.9 1.3 collective-permute-start.1
  20.2 1.4 reshape.40
  24.8 16.9 %fusion.7 = f32[1,224,256]{1,0,2:T(1,128)S(1)} fusion(bf16[1,8,1279]{1,0,2:T(2,128)(2,1)S(1)} %copy.13, s32[224]{0:T(256)S(1)} %copy-done.3, bf16[224,1024]{0,1:T(8,128)(2,1)S(1)} %copy.12), kind=kOutput, calls=%fused_computation.10 | convolution fusion | flops 943194112 | bytes 709488 | tf_op jit(solution)/shard_map/conv_general_dilated | solution.py:74
  42.0 2.9 %collective-permute-start.2 = (bf16[28,4,256]{2,0,1:T(8,128)(2,1)S(1)}, bf16[28,4,256]{2,0,1:T(8,128)(2,1)S(1)}, u32[]{:S(2)}, u32[]{:S(2)}) collective-permute-start(bf16[28,4,256]{2,0,1:T(8,128)(2,1)S(1)} %fusion.13), channel_id=1, source_target_pairs={{0,1},{1,2},{2,3},{3,4},{4,5},{5,6},{6,7},{7,8},{8,9},{9,10},{10,1... | collective-permute-start | bytes 172040 | tf_op jit(solution)/shard_map/ppermute | solution.py:18
  44.9 5.0 %collective-permute-done.2 = bf16[28,4,256]{2,0,1:T(8,128)(2,1)S(1)} collective-permute-done((bf16[28,4,256]{2,0,1:T(8,128)(2,1)S(1)}, bf16[28,4,256]{2,0,1:T(8,128)(2,1)S(1)}, u32[]{:S(2)}, u32[]{:S(2)}) %collective-permute-start.2) | collective-permute-done | bytes 57376 | tf_op jit(solution)/shard_map/ppermute | solution.py:18
  49.8 4.4 %collective-permute-start.10 = (bf16[28,4,256]{2,0,1:T(8,128)(2,1)S(1)}, bf16[28,4,256]{2,0,1:T(8,128)(2,1)S(1)}, u32[]{:S(2)}, u32[]{:S(2)}) collective-permute-start(bf16[28,4,256]{2,0,1:T(8,128)(2,1)S(1)} %fusion.13), channel_id=1, source_target_pairs={{0,15},{1,0},{2,1},{3,2},{4,3},{5,4},{6,5},{7,6},{8,7},{9,8},{10,9... | collective-permute-start | bytes 172040 | tf_op jit(solution)/shard_map/ppermute | solution.py:20
  54.3 1.9 %collective-permute-done.3 = bf16[28,4,256]{2,0,1:T(8,128)(2,1)S(1)} collective-permute-done((bf16[28,4,256]{2,0,1:T(8,128)(2,1)S(1)}, bf16[28,4,256]{2,0,1:T(8,128)(2,1)S(1)}, u32[]{:S(2)}, u32[]{:S(2)}) %collective-permute-start.3) | collective-permute-done | bytes 57376 | tf_op jit(solution)/shard_map/ppermute | solution.py:18
  56.2 4.5 %collective-permute-start.11 = (bf16[28,4,256]{2,0,1:T(8,128)(2,1)S(1)}, bf16[28,4,256]{2,0,1:T(8,128)(2,1)S(1)}, u32[]{:S(2)}, u32[]{:S(2)}) collective-permute-start(bf16[28,4,256]{2,0,1:T(8,128)(2,1)S(1)} %collective-permute-done.10), channel_id=1, source_target_pairs={{0,15},{1,0},{2,1},{3,2},{4,3},{5,4},{6,5},{7,6},{8,7},{9,8},{10,9... | collective-permute-start | bytes 172040 | tf_op jit(solution)/shard_map/ppermute | solution.py:20
  60.7 1.9 %collective-permute-done.4 = bf16[28,4,256]{2,0,1:T(8,128)(2,1)S(1)} collective-permute-done((bf16[28,4,256]{2,0,1:T(8,128)(2,1)S(1)}, bf16[28,4,256]{2,0,1:T(8,128)(2,1)S(1)}, u32[]{:S(2)}, u32[]{:S(2)}) %collective-permute-start.4) | collective-permute-done | bytes 57376 | tf_op jit(solution)/shard_map/ppermute | solution.py:18
  62.6 4.5 %collective-permute-start.12 = (bf16[28,4,256]{2,0,1:T(8,128)(2,1)S(1)}, bf16[28,4,256]{2,0,1:T(8,128)(2,1)S(1)}, u32[]{:S(2)}, u32[]{:S(2)}) collective-permute-start(bf16[28,4,256]{2,0,1:T(8,128)(2,1)S(1)} %collective-permute-done.11), channel_id=1, source_target_pairs={{0,15},{1,0},{2,1},{3,2},{4,3},{5,4},{6,5},{7,6},{8,7},{9,8},{10,9... | collective-permute-start | bytes 172040 | tf_op jit(solution)/shard_map/ppermute | solution.py:20
  67.1 1.9 %collective-permute-done.5 = bf16[28,4,256]{2,0,1:T(8,128)(2,1)S(1)} collective-permute-done((bf16[28,4,256]{2,0,1:T(8,128)(2,1)S(1)}, bf16[28,4,256]{2,0,1:T(8,128)(2,1)S(1)}, u32[]{:S(2)}, u32[]{:S(2)}) %collective-permute-start.5) | collective-permute-done | bytes 57376 | tf_op jit(solution)/shard_map/ppermute | solution.py:18
  69.0 4.5 %collective-permute-start.13 = (bf16[28,4,256]{2,0,1:T(8,128)(2,1)S(1)}, bf16[28,4,256]{2,0,1:T(8,128)(2,1)S(1)}, u32[]{:S(2)}, u32[]{:S(2)}) collective-permute-start(bf16[28,4,256]{2,0,1:T(8,128)(2,1)S(1)} %collective-permute-done.12), channel_id=1, source_target_pairs={{0,15},{1,0},{2,1},{3,2},{4,3},{5,4},{6,5},{7,6},{8,7},{9,8},{10,9... | collective-permute-start | bytes 172040 | tf_op jit(solution)/shard_map/ppermute | solution.py:20
  73.5 1.9 %collective-permute-done.6 = bf16[28,4,256]{2,0,1:T(8,128)(2,1)S(1)} collective-permute-done((bf16[28,4,256]{2,0,1:T(8,128)(2,1)S(1)}, bf16[28,4,256]{2,0,1:T(8,128)(2,1)S(1)}, u32[]{:S(2)}, u32[]{:S(2)}) %collective-permute-start.6) | collective-permute-done | bytes 57376 | tf_op jit(solution)/shard_map/ppermute | solution.py:18
  75.4 4.5 %collective-permute-start.14 = (bf16[28,4,256]{2,0,1:T(8,128)(2,1)S(1)}, bf16[28,4,256]{2,0,1:T(8,128)(2,1)S(1)}, u32[]{:S(2)}, u32[]{:S(2)}) collective-permute-start(bf16[28,4,256]{2,0,1:T(8,128)(2,1)S(1)} %collective-permute-done.13), channel_id=1, source_target_pairs={{0,15},{1,0},{2,1},{3,2},{4,3},{5,4},{6,5},{7,6},{8,7},{9,8},{10,9... | collective-permute-start | bytes 172040 | tf_op jit(solution)/shard_map/ppermute | solution.py:20
  79.9 1.9 %collective-permute-done.7 = bf16[28,4,256]{2,0,1:T(8,128)(2,1)S(1)} collective-permute-done((bf16[28,4,256]{2,0,1:T(8,128)(2,1)S(1)}, bf16[28,4,256]{2,0,1:T(8,128)(2,1)S(1)}, u32[]{:S(2)}, u32[]{:S(2)}) %collective-permute-start.7) | collective-permute-done | bytes 57376 | tf_op jit(solution)/shard_map/ppermute | solution.py:18
  81.9 4.4 %collective-permute-start.15 = (bf16[28,4,256]{2,0,1:T(8,128)(2,1)S(1)}, bf16[28,4,256]{2,0,1:T(8,128)(2,1)S(1)}, u32[]{:S(2)}, u32[]{:S(2)}) collective-permute-start(bf16[28,4,256]{2,0,1:T(8,128)(2,1)S(1)} %collective-permute-done.14), channel_id=1, source_target_pairs={{0,15},{1,0},{2,1},{3,2},{4,3},{5,4},{6,5},{7,6},{8,7},{9,8},{10,9... | collective-permute-start | bytes 172040 | tf_op jit(solution)/shard_map/ppermute | solution.py:20
  86.3 1.9 %collective-permute-done.8 = bf16[28,4,256]{2,0,1:T(8,128)(2,1)S(1)} collective-permute-done((bf16[28,4,256]{2,0,1:T(8,128)(2,1)S(1)}, bf16[28,4,256]{2,0,1:T(8,128)(2,1)S(1)}, u32[]{:S(2)}, u32[]{:S(2)}) %collective-permute-start.8) | collective-permute-done | bytes 57376 | tf_op jit(solution)/shard_map/ppermute | solution.py:18
  88.3 4.5 %collective-permute-start.16 = (bf16[28,4,256]{2,0,1:T(8,128)(2,1)S(1)}, bf16[28,4,256]{2,0,1:T(8,128)(2,1)S(1)}, u32[]{:S(2)}, u32[]{:S(2)}) collective-permute-start(bf16[28,4,256]{2,0,1:T(8,128)(2,1)S(1)} %collective-permute-done.15), channel_id=1, source_target_pairs={{0,15},{1,0},{2,1},{3,2},{4,3},{5,4},{6,5},{7,6},{8,7},{9,8},{10,9... | collective-permute-start | bytes 172040 | tf_op jit(solution)/shard_map/ppermute | solution.py:20
  92.8 1.7 %collective-permute-done.9 = bf16[28,4,256]{2,0,1:T(8,128)(2,1)S(1)} collective-permute-done((bf16[28,4,256]{2,0,1:T(8,128)(2,1)S(1)}, bf16[28,4,256]{2,0,1:T(8,128)(2,1)S(1)}, u32[]{:S(2)}, u32[]{:S(2)}) %collective-permute-start.9) | collective-permute-done | bytes 57376 | tf_op jit(solution)/shard_map/ppermute | solution.py:18
  95.8 28.9 %while.11 = (s32[]{:T(128)}, f32[64,4096]{1,0:T(8,128)S(1)}, bf16[28,64,256]{2,1,0:T(8,128)(2,1)S(1)}, s32[28,4096]{1,0:T(8,128)S(1)}, s32[]{:T(128)}, /*index=5*/s32[]{:T(128)}) while((s32[]{:T(128)}, f32[64,4096]{1,0:T(8,128)S(1)}, bf16[28,64,256]{2,1,0:T(8,128)(2,1)S(1)}, s32[28,4096]{1,0:T(8,128)S(1)}, s32[]{:T(128)}, ...), condition=%wide.region_4.5_spmd.clone, body=%wide.region_3.4_spmd.clone.sunk | while | flops 135790592 | bytes 2179159 | solution.py:105
  125.7 20.6 %reduce-scatter.2.cloned.1.call-done = f32[32,4096]{1,0:T(8,128)} async-done(((f32[64,4096]{1,0:T(8,128)}), f32[32,4096]{1,0:T(8,128)}) %reduce-scatter.2.cloned.1.call-update) | async-done | bytes 524304 | tf_op jit(solution)/shard_map/reduce_scatter | solution.py:113
  146.3 1.9 %broadcast_multiply_fusion = f32[32,4096]{1,0:T(8,128)} fusion(f32[32,4096]{1,0:T(8,128)} %reduce-scatter.2.cloned.1.call-done), kind=kLoop, calls=%fused_computation.17 | loop fusion | flops 131072 | bytes 1048576 | tf_op jit(solution)/shard_map/mul | solution.py:114
  (138 shorter events, 33.5 us)
Async XLA Ops:
  6.5 139.8 %reduce-scatter.2.cloned.1.call-start = ((), (), s32[]{:S(2)}) async-start(), calls=%async_computation.1 | async-start | bytes 1572864 | tf_op jit(solution)/shard_map/reduce_scatter | solution.py:113
  17.6 6.3 %collective-permute-start = (bf16[2,128]{1,0:T(2,128)(2,1)S(1)}, bf16[2,128]{1,0:T(2,128)(2,1)S(1)}, u32[]{:S(2)}, u32[]{:S(2)}) collective-permute-start(bf16[2,128]{1,0:T(2,128)(2,1)S(1)} %get-tuple-element.64), channel_id=1, source_target_pairs={{0,1},{1,2},{2,3},{3,4},{4,5},{5,6},{6,7},{7,8},{8,9},{9,10},{10,1... | collective-permute-start | bytes 1544 | tf_op jit(solution)/shard_map/ppermute | solution.py:35
  18.9 5.0 %collective-permute-start.1 = (bf16[2,128]{1,0:T(2,128)(2,1)S(1)}, bf16[2,128]{1,0:T(2,128)(2,1)S(1)}, u32[]{:S(2)}, u32[]{:S(2)}) collective-permute-start(bf16[2,128]{1,0:T(2,128)(2,1)S(1)} %get-tuple-element.65), channel_id=1, source_target_pairs={{1,0},{2,1},{3,2},{4,3},{5,4},{6,5},{7,6},{8,7},{9,8},{10,9},{11,1... | collective-permute-start | bytes 1544 | tf_op jit(solution)/shard_map/ppermute | solution.py:38
  21.7 3.1 %copy-start.3 = (s32[224]{0:T(256)S(1)}, s32[224]{0:T(256)}, u32[]{:S(2)}) copy-start(s32[224]{0:T(256)} %constant.77.clone.1) | copy-start | bytes 2692
  24.8 57.0 %copy-start.2 = (s32[56]{0:T(128)S(1)}, s32[56]{0:T(128)}, u32[]{:S(2)}) copy-start(s32[56]{0:T(128)} %param.8) | copy-start | bytes 676
  24.8 63.4 %copy-start.1 = (s32[56,4096]{1,0:T(8,128)S(1)}, s32[56,4096]{1,0:T(8,128)}, u32[]{:S(2)}) copy-start(s32[56,4096]{1,0:T(8,128)} %param.7) | copy-start | bytes 2752516
  42.0 7.9 %collective-permute-start.2 = (bf16[28,4,256]{2,0,1:T(8,128)(2,1)S(1)}, bf16[28,4,256]{2,0,1:T(8,128)(2,1)S(1)}, u32[]{:S(2)}, u32[]{:S(2)}) collective-permute-start(bf16[28,4,256]{2,0,1:T(8,128)(2,1)S(1)} %fusion.13), channel_id=1, source_target_pairs={{0,1},{1,2},{2,3},{3,4},{4,5},{5,6},{6,7},{7,8},{8,9},{9,10},{10,1... | collective-permute-start | bytes 172040 | tf_op jit(solution)/shard_map/ppermute | solution.py:18
  49.8 6.4 %collective-permute-start.3 = (bf16[28,4,256]{2,0,1:T(8,128)(2,1)S(1)}, bf16[28,4,256]{2,0,1:T(8,128)(2,1)S(1)}, u32[]{:S(2)}, u32[]{:S(2)}) collective-permute-start(bf16[28,4,256]{2,0,1:T(8,128)(2,1)S(1)} %collective-permute-done.2), channel_id=1, source_target_pairs={{0,1},{1,2},{2,3},{3,4},{4,5},{5,6},{6,7},{7,8},{8,9},{9,10},{10,1... | collective-permute-start | bytes 172040 | tf_op jit(solution)/shard_map/ppermute | solution.py:18
  49.8 6.4 %collective-permute-start.10 = (bf16[28,4,256]{2,0,1:T(8,128)(2,1)S(1)}, bf16[28,4,256]{2,0,1:T(8,128)(2,1)S(1)}, u32[]{:S(2)}, u32[]{:S(2)}) collective-permute-start(bf16[28,4,256]{2,0,1:T(8,128)(2,1)S(1)} %fusion.13), channel_id=1, source_target_pairs={{0,15},{1,0},{2,1},{3,2},{4,3},{5,4},{6,5},{7,6},{8,7},{9,8},{10,9... | collective-permute-start | bytes 172040 | tf_op jit(solution)/shard_map/ppermute | solution.py:20
  56.2 6.4 %collective-permute-start.4 = (bf16[28,4,256]{2,0,1:T(8,128)(2,1)S(1)}, bf16[28,4,256]{2,0,1:T(8,128)(2,1)S(1)}, u32[]{:S(2)}, u32[]{:S(2)}) collective-permute-start(bf16[28,4,256]{2,0,1:T(8,128)(2,1)S(1)} %collective-permute-done.3), channel_id=1, source_target_pairs={{0,1},{1,2},{2,3},{3,4},{4,5},{5,6},{6,7},{7,8},{8,9},{9,10},{10,1... | collective-permute-start | bytes 172040 | tf_op jit(solution)/shard_map/ppermute | solution.py:18
  56.2 6.4 %collective-permute-start.11 = (bf16[28,4,256]{2,0,1:T(8,128)(2,1)S(1)}, bf16[28,4,256]{2,0,1:T(8,128)(2,1)S(1)}, u32[]{:S(2)}, u32[]{:S(2)}) collective-permute-start(bf16[28,4,256]{2,0,1:T(8,128)(2,1)S(1)} %collective-permute-done.10), channel_id=1, source_target_pairs={{0,15},{1,0},{2,1},{3,2},{4,3},{5,4},{6,5},{7,6},{8,7},{9,8},{10,9... | collective-permute-start | bytes 172040 | tf_op jit(solution)/shard_map/ppermute | solution.py:20
  62.6 6.4 %collective-permute-start.5 = (bf16[28,4,256]{2,0,1:T(8,128)(2,1)S(1)}, bf16[28,4,256]{2,0,1:T(8,128)(2,1)S(1)}, u32[]{:S(2)}, u32[]{:S(2)}) collective-permute-start(bf16[28,4,256]{2,0,1:T(8,128)(2,1)S(1)} %collective-permute-done.4), channel_id=1, source_target_pairs={{0,1},{1,2},{2,3},{3,4},{4,5},{5,6},{6,7},{7,8},{8,9},{9,10},{10,1... | collective-permute-start | bytes 172040 | tf_op jit(solution)/shard_map/ppermute | solution.py:18
  62.6 6.4 %collective-permute-start.12 = (bf16[28,4,256]{2,0,1:T(8,128)(2,1)S(1)}, bf16[28,4,256]{2,0,1:T(8,128)(2,1)S(1)}, u32[]{:S(2)}, u32[]{:S(2)}) collective-permute-start(bf16[28,4,256]{2,0,1:T(8,128)(2,1)S(1)} %collective-permute-done.11), channel_id=1, source_target_pairs={{0,15},{1,0},{2,1},{3,2},{4,3},{5,4},{6,5},{7,6},{8,7},{9,8},{10,9... | collective-permute-start | bytes 172040 | tf_op jit(solution)/shard_map/ppermute | solution.py:20
  69.0 6.4 %collective-permute-start.6 = (bf16[28,4,256]{2,0,1:T(8,128)(2,1)S(1)}, bf16[28,4,256]{2,0,1:T(8,128)(2,1)S(1)}, u32[]{:S(2)}, u32[]{:S(2)}) collective-permute-start(bf16[28,4,256]{2,0,1:T(8,128)(2,1)S(1)} %collective-permute-done.5), channel_id=1, source_target_pairs={{0,1},{1,2},{2,3},{3,4},{4,5},{5,6},{6,7},{7,8},{8,9},{9,10},{10,1... | collective-permute-start | bytes 172040 | tf_op jit(solution)/shard_map/ppermute | solution.py:18
  69.0 6.4 %collective-permute-start.13 = (bf16[28,4,256]{2,0,1:T(8,128)(2,1)S(1)}, bf16[28,4,256]{2,0,1:T(8,128)(2,1)S(1)}, u32[]{:S(2)}, u32[]{:S(2)}) collective-permute-start(bf16[28,4,256]{2,0,1:T(8,128)(2,1)S(1)} %collective-permute-done.12), channel_id=1, source_target_pairs={{0,15},{1,0},{2,1},{3,2},{4,3},{5,4},{6,5},{7,6},{8,7},{9,8},{10,9... | collective-permute-start | bytes 172040 | tf_op jit(solution)/shard_map/ppermute | solution.py:20
  75.4 6.4 %collective-permute-start.7 = (bf16[28,4,256]{2,0,1:T(8,128)(2,1)S(1)}, bf16[28,4,256]{2,0,1:T(8,128)(2,1)S(1)}, u32[]{:S(2)}, u32[]{:S(2)}) collective-permute-start(bf16[28,4,256]{2,0,1:T(8,128)(2,1)S(1)} %collective-permute-done.6), channel_id=1, source_target_pairs={{0,1},{1,2},{2,3},{3,4},{4,5},{5,6},{6,7},{7,8},{8,9},{9,10},{10,1... | collective-permute-start | bytes 172040 | tf_op jit(solution)/shard_map/ppermute | solution.py:18
  75.4 6.4 %collective-permute-start.14 = (bf16[28,4,256]{2,0,1:T(8,128)(2,1)S(1)}, bf16[28,4,256]{2,0,1:T(8,128)(2,1)S(1)}, u32[]{:S(2)}, u32[]{:S(2)}) collective-permute-start(bf16[28,4,256]{2,0,1:T(8,128)(2,1)S(1)} %collective-permute-done.13), channel_id=1, source_target_pairs={{0,15},{1,0},{2,1},{3,2},{4,3},{5,4},{6,5},{7,6},{8,7},{9,8},{10,9... | collective-permute-start | bytes 172040 | tf_op jit(solution)/shard_map/ppermute | solution.py:20
  81.8 6.4 %collective-permute-start.8 = (bf16[28,4,256]{2,0,1:T(8,128)(2,1)S(1)}, bf16[28,4,256]{2,0,1:T(8,128)(2,1)S(1)}, u32[]{:S(2)}, u32[]{:S(2)}) collective-permute-start(bf16[28,4,256]{2,0,1:T(8,128)(2,1)S(1)} %collective-permute-done.7), channel_id=1, source_target_pairs={{0,1},{1,2},{2,3},{3,4},{4,5},{5,6},{6,7},{7,8},{8,9},{9,10},{10,1... | collective-permute-start | bytes 172040 | tf_op jit(solution)/shard_map/ppermute | solution.py:18
  81.9 6.5 %collective-permute-start.15 = (bf16[28,4,256]{2,0,1:T(8,128)(2,1)S(1)}, bf16[28,4,256]{2,0,1:T(8,128)(2,1)S(1)}, u32[]{:S(2)}, u32[]{:S(2)}) collective-permute-start(bf16[28,4,256]{2,0,1:T(8,128)(2,1)S(1)} %collective-permute-done.14), channel_id=1, source_target_pairs={{0,15},{1,0},{2,1},{3,2},{4,3},{5,4},{6,5},{7,6},{8,7},{9,8},{10,9... | collective-permute-start | bytes 172040 | tf_op jit(solution)/shard_map/ppermute | solution.py:20
  88.2 6.4 %collective-permute-start.9 = (bf16[28,4,256]{2,0,1:T(8,128)(2,1)S(1)}, bf16[28,4,256]{2,0,1:T(8,128)(2,1)S(1)}, u32[]{:S(2)}, u32[]{:S(2)}) collective-permute-start(bf16[28,4,256]{2,0,1:T(8,128)(2,1)S(1)} %collective-permute-done.8), channel_id=1, source_target_pairs={{0,1},{1,2},{2,3},{3,4},{4,5},{5,6},{6,7},{7,8},{8,9},{9,10},{10,1... | collective-permute-start | bytes 172040 | tf_op jit(solution)/shard_map/ppermute | solution.py:18
  88.3 6.5 %collective-permute-start.16 = (bf16[28,4,256]{2,0,1:T(8,128)(2,1)S(1)}, bf16[28,4,256]{2,0,1:T(8,128)(2,1)S(1)}, u32[]{:S(2)}, u32[]{:S(2)}) collective-permute-start(bf16[28,4,256]{2,0,1:T(8,128)(2,1)S(1)} %collective-permute-done.15), channel_id=1, source_target_pairs={{0,15},{1,0},{2,1},{3,2},{4,3},{5,4},{6,5},{7,6},{8,7},{9,8},{10,9... | collective-permute-start | bytes 172040 | tf_op jit(solution)/shard_map/ppermute | solution.py:20
  124.7 1.0 copy-start
Sparse Core Ops, SparseCore 0:
  125.8 20.4 reduce-scatter.1
